TPU v7x, 256 devices: a whole 4x4x8 slice. The times are simulated.
256 devices in a mesh: scene: 128 (over x_lo, y, z, core), tile: 2 (over x_hi).
Axes of the slice: x: 4 (x_hi: 2, x_lo: 2; x = x_hi * 2 + x_lo), y: 4, z: 8, core: 2. Of those that a mesh axis runs over, the one named last changes fastest.
Arguments:
- features_in: bfloat16 [128, 4, 64, 4096], P('scene', 'tile'), may hold values from -6 to 6
- strided_weights: bfloat16 [2, 64, 1024], replicated, may hold values from -0.1875 to 0.1875
- dilated_weights: bfloat16 [2, 64, 576], replicated, may hold values from -0.25 to 0.25
- tile_bias: float32 [256, 64], replicated, may hold values from -3 to 3
- cost_cotangent: bfloat16 [128, 4, 1024], P('scene', 'tile'), may hold values from -6 to 6
- footprint_pairing: int32 [64, 4], replicated, may hold values from 0 to 3, each once within a row
- valid_counts: int32 [64], replicated, may hold values from 1 to 4, as said below
- tile_owner: int32 [128], replicated, may hold values from 0 to 255, as said below
Outputs:
- grad_features: bfloat16 [128, 4, 64, 4096], P('scene', 'tile')
- grad_weights: float32 [128, 1600], P('scene')
- grad_bias: float32 [256, 64], P(('scene', 'tile'))
Inputs may be any that keep to these rules, and one draw needn't show every extreme that they name: `footprint_pairing`: row k maps each patch of scene 2k to the patch of scene 2k + 1 that covers its footprint; each row is a permutation. `valid_counts`: patches 0 to count - 1 of both scenes of a pair are live; some pair has all 4 live. `tile_owner`: several scenes may share a tile, and many tiles have no scene.
All inputs are finite; a program needn't handle non-finite values.
Results may differ from a plain program's by a relative error of at most 0.007.
Values may be sent and summed in bfloat16 or wider, within the bound.
A program may use at most 64 MiB of HBM per device.

v0:
```python
import math
import jax
import jax.numpy as jnp
from jax import lax
from jax.sharding import PartitionSpec as P


def from_partner(x, axis, distance):
    return lax.ppermute(x, axis, [(i, i ^ 1 << distance) for i in range(lax.axis_size(axis))])


def apply_convolution(
    left_operand,
    right_operand,
    window_strides,
    border_padding,
    left_dilation,
    right_dilation,
    dimension_labels,
):
    return lax.conv_general_dilated(
        left_operand,
        right_operand,
        window_strides,
        border_padding,
        lhs_dilation=left_dilation,
        rhs_dilation=right_dilation,
        dimension_numbers=dimension_labels,
        preferred_element_type=jnp.float32,
    )


def silu_slope(pre_act):
    sigmoid_gate = jax.nn.sigmoid(pre_act)
    return sigmoid_gate * (1.0 + pre_act * (1.0 - sigmoid_gate))


def match_rows(pairing_row, branch, first_patch, patch_count):
    total_patches = pairing_row.shape[0]
    all_patches = jnp.arange(total_patches, dtype=jnp.int32)
    inverse = jnp.sum(
        jnp.where(pairing_row[:, None] == all_patches[None, :], all_patches[:, None], 0), axis=0
    )
    positions = first_patch + jnp.arange(patch_count, dtype=jnp.int32)
    return jnp.where(branch == 0, jnp.take(pairing_row, positions), jnp.take(inverse, positions))


def local(
    features_in,
    strided_weights,
    dilated_weights,
    tile_bias,
    cost_cotangent,
    footprint_pairing,
    valid_counts,
    tile_owner,
):
    scene_index = lax.axis_index("scene")
    tile_index = lax.axis_index("tile")
    branch = scene_index % 2
    pair_index = scene_index // 2
    features = features_in[0]
    own_cotangent = cost_cotangent[0]
    patches, channels, cells_in = (features.shape[0], features.shape[1], features.shape[2])
    cells_out = own_cotangent.shape[1]
    grid_side = math.isqrt(cells_in)
    half_side = grid_side // 2
    strided_kernel = lax.dynamic_index_in_dim(strided_weights, branch, 0, keepdims=False).reshape(
        channels, channels, 4, 4
    )
    dilated_kernel = lax.dynamic_index_in_dim(dilated_weights, branch, 0, keepdims=False).reshape(
        channels, channels, 3, 3
    )
    tile_id = lax.dynamic_index_in_dim(tile_owner, scene_index, 0, keepdims=False)
    bias_row = lax.dynamic_index_in_dim(tile_bias, tile_id, 0, keepdims=False)
    plain = ("NCHW", "OIHW", "NCHW")
    flipped = ("NCHW", "IOHW", "NCHW")
    kernel_side = ("CNHW", "IOHW", "CNHW")
    feature_grid = features.reshape(patches, channels, grid_side, grid_side)
    pre_act = (
        apply_convolution(
            feature_grid, strided_kernel, (2, 2), ((1, 1), (1, 1)), (1, 1), (1, 1), plain
        )
        + bias_row[None, :, None, None]
    )
    activation = jax.nn.silu(pre_act).astype(jnp.bfloat16)
    branch_grid = apply_convolution(
        activation, dilated_kernel, (1, 1), ((2, 2), (2, 2)), (1, 1), (2, 2), plain
    ).astype(jnp.bfloat16)
    branch_out = branch_grid.reshape(patches, channels, cells_out)
    pairing_row = lax.dynamic_index_in_dim(footprint_pairing, pair_index, 0, keepdims=False)
    first_patch = tile_index * patches
    swapped_out, swapped_cot = from_partner((branch_out, own_cotangent), "scene", 0)
    partner_out, partner_cot = (
        lax.all_gather(swapped_out, "tile", axis=0, tiled=True),
        lax.all_gather(swapped_cot, "tile", axis=0, tiled=True),
    )
    matched = match_rows(pairing_row, branch, first_patch, patches)
    chosen_out = jnp.take(partner_out, matched, axis=0)
    chosen_cot = jnp.take(partner_cot, matched, axis=0)
    pair_valid = lax.dynamic_index_in_dim(valid_counts, pair_index, 0, keepdims=False)
    live_count = jnp.clip(pair_valid - first_patch, 0, patches)
    live_mask = (jnp.arange(patches, dtype=jnp.int32) < live_count).astype(jnp.float32)
    signal = (own_cotangent.astype(jnp.float32) + chosen_cot.astype(jnp.float32)) * live_mask[
        :, None
    ]
    out_grad = (signal[:, None, :] * chosen_out.astype(jnp.float32)).astype(jnp.bfloat16)
    out_grid = out_grad.reshape(patches, channels, half_side, half_side)
    act_grad = apply_convolution(
        out_grid,
        dilated_kernel[:, :, ::-1, ::-1],
        (1, 1),
        ((2, 2), (2, 2)),
        (1, 1),
        (2, 2),
        flipped,
    )
    grad_dilated = apply_convolution(
        activation, out_grid, (2, 2), ((2, 2), (2, 2)), (1, 1), (1, 1), kernel_side
    )
    pre_grad = act_grad * silu_slope(pre_act)
    bias_grad = jnp.sum(pre_grad, axis=(0, 2, 3))
    pre_narrow = pre_grad.astype(jnp.bfloat16)
    grad_strided = apply_convolution(
        feature_grid, pre_narrow, (1, 1), ((1, 1), (1, 1)), (1, 1), (2, 2), kernel_side
    )
    feature_grad = apply_convolution(
        pre_narrow,
        strided_kernel[:, :, ::-1, ::-1],
        (1, 1),
        ((2, 2), (2, 2)),
        (2, 2),
        (1, 1),
        flipped,
    )
    feature_grads = feature_grad.astype(jnp.bfloat16).reshape(patches, channels, cells_in)
    grad_row = jnp.concatenate(
        [
            grad_strided.reshape(channels, 16 * channels),
            grad_dilated.reshape(channels, 9 * channels),
        ],
        axis=1,
    )
    scenes = lax.axis_size("scene")
    tile_devices = lax.axis_size("tile")
    weight_scale = 1.0 / math.sqrt(scenes * patches * tile_devices * cells_out)
    bias_scale = 1.0 / math.sqrt(patches * tile_devices * cells_out)
    branch_hit = jnp.arange(2, dtype=jnp.int32)[:, None, None] == branch
    weight_term = jnp.where(branch_hit, (grad_row * weight_scale)[None], jnp.float32(0.0)).reshape(
        2 * channels, 25 * channels
    )
    rows_each = 2 * channels // scenes
    summed = lax.psum(weight_term, ("scene", "tile"))
    grad_weights = lax.dynamic_slice_in_dim(summed, scene_index * rows_each, rows_each, 0)
    bias_rows = tile_bias.shape[0] // (scenes * tile_devices)
    scaled_bias = bias_grad * bias_scale
    owned_mask = tile_id == jnp.arange(
        lax.axis_size(("scene", "tile")) * bias_rows, dtype=jnp.int32
    )
    grad_bias = lax.psum_scatter(
        jnp.where(owned_mask[:, None], scaled_bias[None, :], jnp.float32(0.0)),
        ("scene", "tile"),
        scatter_dimension=0,
        tiled=True,
    )
    return (feature_grads[None], grad_weights, grad_bias)


def solution(mesh):
    return jax.shard_map(
        local,
        mesh=mesh,
        in_specs=(
            P("scene", "tile", None, None),
            P(),
            P(),
            P(),
            P("scene", "tile", None),
            P(),
            P(),
            P(),
        ),
        out_specs=(P("scene", "tile", None, None), P("scene", None), P(("scene", "tile"), None)),
        check_vma=False,
    )
```

profile of v0, /device:TPU:2, one launch (start us, length us, event | category | flops | bytes accessed | tf_op | source)
XLA Modules:
  0.0 381.2 jit_solution(3628517353644582072)
XLA Ops:
  7.4 1.3 dynamic_slice.30
  10.0 0.9 constant_dynamic-slice_fusion.1
  11.2 0.8 copy.171
  12.2 1.0 copy.169
  13.2 2.3 reshape_squeeze.3
  15.4 2.9 copy.200
  18.3 3.4 fusion.59
  21.8 2.7 fusion.12
  24.5 6.3 %copy.167 = bf16[64,64,2,8,13]{0,3,2,4,1:T(8,128)(2,1)} copy(bf16[64,64,2,8,13]{1,0,4,3,2:T(8,128)(2,1)} %fusion.12) | data formatting | bytes 3407872 | tf_op jit(solution)/shard_map/conv_general_dilated | solution.py:21
  31.6 4.8 %fusion.27 = f32[32,16,5,64]{3,1,2,0:T(8,128)S(1)} fusion(bf16[64,64,4,4]{1,0,3,2:T(8,128)(2,1)S(1)} %copy-done.11, bf16[64,64,2,8,13]{0,3,2,4,1:T(8,128)(2,1)} %copy.167, f32[64]{0:T(128)S(1)} %dynamic-slice_reduce_fusion, pred[16,5]{0,1:T(8,128)(4,1)S(1)} %copy-done.17), kind=kOutput, calls=%fused_computation.39 | convolution fusion | flops 330629120 | bytes 2490704 | tf_op jit(solution)/shard_map/conv_general_dilated | solution.py:21
  36.5 0.5 select_bitcast_fusion
  37.5 1.7 convolution_convert_fusion.1
  39.5 1.0 copy.173
  40.8 1.2 iota_compare_fusion.9
  42.0 0.8 fusion.58
  42.8 3.6 fusion.57
  46.4 0.6 dynamic_slice.28
  47.9 0.6 gather_fusion.2
  48.6 0.6 gather_fusion.3
  49.2 4.2 %fusion.15 = (bf16[64,64,2,8,10]{1,0,4,3,2:T(8,128)(2,1)}, bf16[64,64,2,8,10]{1,0,4,3,2:T(8,128)(2,1)S(1)}) fusion(bf16[64,64,2,7,1]{1,0,4,3,2:T(8,128)(2,1)} %get-tuple-element.12, bf16[64,64,2,8,9]{1,0,4,3,2:T(8,128)(2,1)} %get-tuple-element.10, bf16[64,64,2,7,1]{1,0,4,3,2:T(8,128)(2,1)} %get-tuple-element.14, bf16[64,64,2,8,9]{1,0,4,3,2:T(8,128)(2,1)} %get-tuple-element.11), kind=kLoop, calls=%fused_computation.22 | loop fusion | flops 7864320 | bytes 5210112 | tf_op jit(solution)/shard_map/reshape;squeeze | solution.py:79
  53.4 0.7 slice.38
  54.2 0.9 copy-done.2
  55.1 2.3 fusion.17
  57.5 4.6 %copy.187 = bf16[64,64,2,8,10]{0,3,2,4,1:T(8,128)(2,1)} copy(bf16[64,64,2,8,10]{1,0,4,3,2:T(8,128)(2,1)} %copy-done.2) | data formatting | bytes 2621440 | tf_op jit(solution)/shard_map/reshape;squeeze | solution.py:79
  62.2 0.6 broadcast_in_dim.101
  63.0 2.9 copy.189
  66.0 4.8 %copy.185 = bf16[64,64,2,8,10]{0,3,2,4,1:T(8,128)(2,1)} copy(bf16[64,64,2,8,10]{1,0,4,3,2:T(8,128)(2,1)} %get-tuple-element.23) | data formatting | bytes 2621440 | tf_op jit(solution)/shard_map/reshape;squeeze | solution.py:79
  70.8 2.9 copy.188
  73.7 5.9 %all-gather = bf16[2,2,1024]{2,1,0:T(2,128)(2,1)S(1)} all-gather(bf16[1,2,1024]{2,1,0:T(2,128)(2,1)S(1)} %bitcast.88), channel_id=1, replica_groups=mesh['scene'=128,'tile'=2] {'tile'}, dimensions={0}, use_global_device_ids=true | all-gather | bytes 12288 | tf_op jit(solution)/shard_map/all_gather | solution.py:96
  79.6 0.6 gather_fusion
  80.3 1.2 copy.174
  81.6 9.4 %all_gather.7 = bf16[4,64,1024]{2,1,0:T(8,128)(2,1)S(1)} all-gather(bf16[2,64,1024]{2,1,0:T(8,128)(2,1)S(1)} %copy.174), channel_id=1, replica_groups=mesh['scene'=128,'tile'=2] {'tile'}, dimensions={0}, use_global_device_ids=true | all-gather | bytes 786432 | tf_op jit(solution)/shard_map/all_gather | solution.py:95
  90.9 0.6 gather_fusion.1
  92.7 3.1 fusion.49
  96.7 0.7 copy-done.9
  97.5 1.5 convert_select_fusion
  100.0 0.8 copy-done.7
  100.8 1.0 copy-done.4
  101.7 5.0 %fusion = f32[64,64,4,4,1]{0,1,3,4,2:T(8,128)S(1)} fusion(bf16[64,64,16,10,1]{0,2,4,3,1:T(8,128)(2,1)S(1)} %bitcast.81, bf16[64,64,16,10,1]{0,2,4,3,1:T(8,128)(2,1)S(1)} %bitcast.79, bf16[64,64,16,10,1]{0,2,4,3,1:T(8,128)(2,1)S(1)} %copy-done.5, bf16[64,64,16,10,1]{0,2,4,3,1:T(8,128)(2,1)S(1)} %bitcast.80, bf16[32,16,5,64]{3,1,2,0:T(8,128)(2,1)S(1)} %get-tuple-element.21), kind=kOutput, calls=%fused_computation.4 | convolution fusion | flops 351272960 | bytes 5832704 | tf_op jit(solution)/shard_map/conv_general_dilated | solution.py:21
  107.3 0.7 broadcast_select_fusion
  108.3 1.1 bitcast_select_fusion
  109.4 3.1 convolution_convert_fusion
  112.5 0.5 copy.182
  113.0 2.9 copy.183
  116.0 4.1 %broadcast_in_dim_reshape.3 = bf16[1,2,64,4096]{3,2,1,0:T(8,128)(2,1)} reshape(bf16[2,64,64,64]{3,2,1,0:T(8,128)(2,1)} %copy.183) | data formatting | bytes 2097152 | tf_op jit(solution)/shard_map/broadcast_in_dim;reshape | solution.py:166
  120.1 251.6 %all-reduce.4.cloned.1.call-done = (f32[128,1600]{1,0:T(8,128)}, f32[256,64]{1,0:T(8,128)}) async-done(((f32[128,1600]{1,0:T(8,128)}, f32[256,64]{1,0:T(8,128)}), (f32[128,1600]{1,0:T(8,128)}, f32[256,64]{1,0:T(8,128)})) %all-reduce.4.cloned.1.call-update) | async-done | bytes 884752 | tf_op jit(solution)/shard_map/psum | solution.py:153
  371.7 1.4 constant_dynamic-slice_fusion
  373.1 1.2 constant_dynamic-slice_fusion.3
  (89 shorter events, 6.7 us)
Async XLA Ops:
  7.2 4.8 %copy-start = (bf16[2,64,1024]{2,1,0:T(8,128)(2,1)S(1)}, bf16[2,64,1024]{2,1,0:T(8,128)(2,1)}, u32[]{:S(2)}) copy-start(bf16[2,64,1024]{2,1,0:T(8,128)(2,1)} %param.11) | copy-start | bytes 786436
  7.2 6.0 %copy-start.10 = (bf16[1,2,64,4096]{3,2,1,0:T(8,128)(2,1)S(1)}, bf16[1,2,64,4096]{3,2,1,0:T(8,128)(2,1)}, u32[]{:S(2)}) copy-start(bf16[1,2,64,4096]{3,2,1,0:T(8,128)(2,1)} %param.10) | copy-start | bytes 3145732
  7.2 364.5 %all-reduce.4.cloned.1.call-start = ((), (), s32[]{:S(2)}) async-start(), calls=%async_computation | async-start | bytes 1966080 | tf_op jit(solution)/shard_map/psum | solution.py:153
  7.2 66.5 %collective-permute-start = (bf16[2,1024]{1,0:T(2,128)(2,1)}, bf16[2,1024]{1,0:T(2,128)(2,1)S(1)}, u32[]{:S(2)}, u32[]{:S(2)}) collective-permute-start(bf16[2,1024]{1,0:T(2,128)(2,1)} %bitcast.87), channel_id=1, source_target_pairs={{0,2},{2,0},{4,6},{6,4},{8,10},{10,8},{12,14},{14,12},{16,18},{18,... | collective-permute-start | bytes 12296 | tf_op jit(solution)/shard_map/ppermute | solution.py:9
  24.5 7.0 %copy-start.15 = (f32[256,64]{0,1:T(8,128)S(1)}, f32[256,64]{0,1:T(8,128)}, u32[]{:S(2)}) copy-start(f32[256,64]{0,1:T(8,128)} %param.13) | copy-start | bytes 196612
  24.5 7.2 %copy-start.11 = (bf16[64,64,4,4]{1,0,3,2:T(8,128)(2,1)S(1)}, bf16[64,64,4,4]{1,0,3,2:T(8,128)(2,1)}, u32[]{:S(2)}) copy-start(bf16[64,64,4,4]{1,0,3,2:T(8,128)(2,1)} %copy.169) | copy-start | bytes 393220
  24.5 7.2 %copy-start.17 = (pred[16,5]{0,1:T(8,128)(4,1)S(1)}, pred[16,5]{0,1:T(8,128)(4,1)}, u32[]{:S(2)}) copy-start(pred[16,5]{0,1:T(8,128)(4,1)} %constant.131) | copy-start | bytes 244
  36.4 2.8 copy-start.8
  36.5 1.1 copy-start.13
  40.5 39.9 %collective-permute-start.1 = (bf16[2,64,1024]{1,2,0:T(8,128)(2,1)}, bf16[2,64,1024]{1,2,0:T(8,128)(2,1)}, u32[]{:S(2)}, u32[]{:S(2)}) collective-permute-start(bf16[2,64,1024]{1,2,0:T(8,128)(2,1)} %bitcast.12), channel_id=1, source_target_pairs={{0,2},{2,0},{4,6},{6,4},{8,10},{10,8},{12,14},{14,12},{16,18},{18,... | collective-permute-start | bytes 786440 | tf_op jit(solution)/shard_map/ppermute | solution.py:9
  42.8 3.6 copy-start.21
  42.8 4.8 %copy-start.18 = (s32[64,4]{0,1:T(4,128)S(1)}, s32[64,4]{0,1:T(4,128)}, u32[]{:S(2)}) copy-start(s32[64,4]{0,1:T(4,128)} %param.15) | copy-start | bytes 3076
  53.4 1.6 copy-start.2
  55.1 2.3 copy-start.16
  66.0 4.8 %copy-start.3 = (bf16[64,64,2,8,10]{1,0,4,3,2:T(8,128)(2,1)S(1)}, bf16[64,64,2,8,10]{1,0,4,3,2:T(8,128)(2,1)}, u32[]{:S(2)}) copy-start(bf16[64,64,2,8,10]{1,0,4,3,2:T(8,128)(2,1)} %fusion.17) | copy-start | bytes 3932164
  96.1 1.3 copy-start.9
  96.1 1.3 copy-start.14
  97.4 2.2 copy-start.5
  97.4 2.5 copy-start.6
  97.4 3.3 copy-start.7
  98.9 2.8 copy-start.4
  101.7 5.5 %copy-start.19 = (pred[256]{0:T(512)(128)(4,1)S(1)}, pred[256]{0:T(512)(128)(4,1)}, u32[]{:S(2)}) copy-start(pred[256]{0:T(512)(128)(4,1)} %iota_compare_fusion.9) | copy-start | bytes 772
  106.7 1.5 copy-start.20
  108.0 1.3 copy-start.12
  113.0 261.3 %copy-start.1 = (bf16[2,64,1024]{2,1,0:T(8,128)(2,1)S(1)}, bf16[2,64,1024]{2,1,0:T(8,128)(2,1)}, u32[]{:S(2)}) copy-start(bf16[2,64,1024]{2,1,0:T(8,128)(2,1)} %param.11) | copy-start | bytes 786436
Sparse Core Ops, SparseCore 0:
  109.5 262.1 all-reduce.3
where the time goes:
time: 382 us; the launch traced here: 381 us
  waiting for transfers between devices  252 us (66%)
  local copies, waits for them, and re-layouts  63.1 us (17%)
  matrix products  19.1 us (5%)
  between operations  17.1 us (4%)
  blocking collectives  15.2 us (4%)
  other arithmetic  14.5 us (4%)
    psum x1, waiting for transfers between devices, local(): summed = lax.psum(weight_term, ('scene', 'tile'))  252 us
    another operation x9, local copies, waits for them, and re-layouts, local(): feature_grid = features.reshape(patches, channels, grid_side, grid_side)  26 us
    conv_general_dilated x6, matrix products, apply_convolution(): lax.conv_general_dilated(left_operand, right_operand, window_strides, bor...  19.1 us
    all_gather x1, blocking collectives, local(): lax.all_gather(swapped_out, 'tile', axis=0, tiled=True)  9.36 us
    unnamed x49, local copies, waits for them, and re-layouts  8.82 us
  transfers between devices with their start and end apart: 3, of which 1 were waited for; matrix products, arithmetic and copies ran while one was open for 19% of the time, Pallas kernels for 0%

commit v1 on v0

--- a/solution.py
+++ b/solution.py
@@ -92,7 +92,9 @@
     first_patch = tile_index * patches
     swapped_out, swapped_cot = from_partner((branch_out, own_cotangent), "scene", 0)
     partner_out, partner_cot = (
-        lax.all_gather(swapped_out, "tile", axis=0, tiled=True),
+        jnp.concatenate(
+            lax.all_to_all(jnp.stack([swapped_out] * lax.axis_size("tile")), "tile", 0, 0), axis=0
+        ),
         lax.all_gather(swapped_cot, "tile", axis=0, tiled=True),
     )
     matched = match_rows(pairing_row, branch, first_patch, patches)

time: 382 us -> 382 us (level)
  blocking collectives: 15.2 us -> 5.85 us
  starting transfers between devices: 0.51 us -> 4.75 us
    all_gather x1 -> x0, blocking collectives: 9.36 us -> none  [local(): lax.all_gather(swapped_out, 'tile', axis=0, tiled=True)]
    all_to_all x0 -> x1, starting transfers between devices: none -> 4.22 us  [local(): lax.all_to_all(jnp.stack([swapped_out] * lax.axis_size('tile')), 'tile',...]
  transfers between devices with their start and end apart: 3 -> 4, of which waited for: 1 -> 1; matrix products, arithmetic and copies ran while one was open for 19% -> 20% of each run, Pallas kernels for 0% -> 0%
where the time goes in v1:
time: 382 us
  waiting for transfers between devices  253 us (66%)
  local copies, waits for them, and re-layouts  65.3 us (17%)
  matrix products  19.1 us (5%)
  between operations  17.2 us (5%)
  other arithmetic  16.8 us (4%)
  blocking collectives  5.85 us (2%)
  starting transfers between devices  4.75 us (1%)
    psum x1, waiting for transfers between devices, local(): summed = lax.psum(weight_term, ('scene', 'tile'))  253 us
    another operation x9, local copies, waits for them, and re-layouts, local(): feature_grid = features.reshape(patches, channels, grid_side, grid_side)  26.1 us
    conv_general_dilated x6, matrix products, apply_convolution(): lax.conv_general_dilated(left_operand, right_operand, window_strides, bor...  19.1 us
    unnamed x49, local copies, waits for them, and re-layouts  8.82 us
  transfers between devices with their start and end apart: 4, of which 1 were waited for; matrix products, arithmetic and copies ran while one was open for 20% of the time, Pallas kernels for 0%

profile of v1, /device:TPU:2, one launch (start us, length us, event | category | flops | bytes accessed | tf_op | source)
XLA Modules:
  0.0 381.6 jit_solution(12697085395429368156)
XLA Ops:
  7.3 1.3 dynamic_slice.30
  9.9 0.9 constant_dynamic-slice_fusion.1
  11.1 0.8 copy.171
  12.1 1.0 copy.169
  13.1 2.3 reshape_squeeze.3
  15.4 2.9 copy.200
  18.3 3.4 fusion.59
  21.7 2.7 fusion.12
  24.4 6.3 %copy.167 = bf16[64,64,2,8,13]{0,3,2,4,1:T(8,128)(2,1)} copy(bf16[64,64,2,8,13]{1,0,4,3,2:T(8,128)(2,1)} %fusion.12) | data formatting | bytes 3407872 | tf_op jit(solution)/shard_map/conv_general_dilated | solution.py:21
  31.5 4.8 %fusion.27 = f32[32,16,5,64]{3,1,2,0:T(8,128)S(1)} fusion(bf16[64,64,4,4]{1,0,3,2:T(8,128)(2,1)S(1)} %copy-done.11, bf16[64,64,2,8,13]{0,3,2,4,1:T(8,128)(2,1)} %copy.167, f32[64]{0:T(128)S(1)} %dynamic-slice_reduce_fusion, pred[16,5]{0,1:T(8,128)(4,1)S(1)} %copy-done.17), kind=kOutput, calls=%fused_computation.39 | convolution fusion | flops 330629120 | bytes 2490704 | tf_op jit(solution)/shard_map/conv_general_dilated | solution.py:21
  37.4 1.7 convolution_convert_fusion.1
  39.3 1.0 copy.173
  40.7 0.8 fusion.58
  41.6 3.6 fusion.57
  45.2 0.6 dynamic_slice.28
  46.7 0.6 gather_fusion.2
  47.4 0.6 gather_fusion.3
  48.0 4.2 %fusion.15 = (bf16[64,64,2,8,10]{1,0,4,3,2:T(8,128)(2,1)}, bf16[64,64,2,8,10]{1,0,4,3,2:T(8,128)(2,1)S(1)}) fusion(bf16[64,64,2,7,1]{1,0,4,3,2:T(8,128)(2,1)} %get-tuple-element.12, bf16[64,64,2,8,9]{1,0,4,3,2:T(8,128)(2,1)} %get-tuple-element.10, bf16[64,64,2,7,1]{1,0,4,3,2:T(8,128)(2,1)} %get-tuple-element.14, bf16[64,64,2,8,9]{1,0,4,3,2:T(8,128)(2,1)} %get-tuple-element.11), kind=kLoop, calls=%fused_computation.22 | loop fusion | flops 7864320 | bytes 5210112 | tf_op jit(solution)/shard_map/reshape;squeeze | solution.py:79
  52.3 0.7 slice.38
  53.0 0.9 copy-done.2
  53.9 1.2 iota_compare_fusion.9
  55.0 2.2 fusion.17
  57.3 2.4 pad_maximum_fusion
  59.7 2.3 copy.174
  62.0 4.2 %all-to-all-start = ((bf16[2,2,64,1024]{3,2,1,0:T(8,128)(2,1)}), bf16[2,2,64,1024]{3,2,1,0:T(8,128)(2,1)}, u32[]{:S(2)}, u32[]{:S(2)}) async-start(bf16[2,2,64,1024]{3,2,1,0:T(8,128)(2,1)} %copy.174), calls=%async_computation | async-start | bytes 1048576 | tf_op jit(solution)/shard_map/all_to_all | solution.py:96
  66.4 4.7 %copy.187 = bf16[64,64,2,8,10]{0,3,2,4,1:T(8,128)(2,1)} copy(bf16[64,64,2,8,10]{1,0,4,3,2:T(8,128)(2,1)} %copy-done.2) | data formatting | bytes 2621440 | tf_op jit(solution)/shard_map/reshape;squeeze | solution.py:79
  71.1 0.6 broadcast_in_dim.101
  72.0 3.0 copy.189
  74.9 4.8 %copy.185 = bf16[64,64,2,8,10]{0,3,2,4,1:T(8,128)(2,1)} copy(bf16[64,64,2,8,10]{1,0,4,3,2:T(8,128)(2,1)} %get-tuple-element.23) | data formatting | bytes 2621440 | tf_op jit(solution)/shard_map/reshape;squeeze | solution.py:79
  79.7 2.9 copy.188
  82.6 5.9 %all-gather = bf16[2,2,1024]{2,1,0:T(2,128)(2,1)S(1)} all-gather(bf16[1,2,1024]{2,1,0:T(2,128)(2,1)S(1)} %bitcast.90), channel_id=1, replica_groups=mesh['scene'=128,'tile'=2] {'tile'}, dimensions={0}, use_global_device_ids=true | all-gather | bytes 12288 | tf_op jit(solution)/shard_map/all_gather | solution.py:98
  88.5 0.6 gather_fusion
  89.3 1.6 gather_fusion.1
  92.1 3.1 fusion.49
  96.1 0.7 copy-done.9
  96.8 1.5 convert_select_fusion
  99.4 0.8 copy-done.7
  100.1 1.0 copy-done.4
  101.1 5.0 %fusion = f32[64,64,4,4,1]{0,1,3,4,2:T(8,128)S(1)} fusion(bf16[64,64,16,10,1]{0,2,4,3,1:T(8,128)(2,1)S(1)} %bitcast.83, bf16[64,64,16,10,1]{0,2,4,3,1:T(8,128)(2,1)S(1)} %bitcast.81, bf16[64,64,16,10,1]{0,2,4,3,1:T(8,128)(2,1)S(1)} %copy-done.5, bf16[64,64,16,10,1]{0,2,4,3,1:T(8,128)(2,1)S(1)} %bitcast.82, bf16[32,16,5,64]{3,1,2,0:T(8,128)(2,1)S(1)} %get-tuple-element.21), kind=kOutput, calls=%fused_computation.4 | convolution fusion | flops 351272960 | bytes 5832704 | tf_op jit(solution)/shard_map/conv_general_dilated | solution.py:21
  106.7 0.7 broadcast_select_fusion
  107.7 1.1 bitcast_select_fusion
  108.8 3.1 convolution_convert_fusion
  111.9 0.5 copy.182
  112.4 2.9 copy.183
  115.4 4.1 %broadcast_in_dim_reshape.3 = bf16[1,2,64,4096]{3,2,1,0:T(8,128)(2,1)} reshape(bf16[2,64,64,64]{3,2,1,0:T(8,128)(2,1)} %copy.183) | data formatting | bytes 2097152 | tf_op jit(solution)/shard_map/broadcast_in_dim;reshape | solution.py:168
  119.5 252.7 %all-reduce.4.cloned.1.call-done = (f32[128,1600]{1,0:T(8,128)}, f32[256,64]{1,0:T(8,128)}) async-done(((f32[128,1600]{1,0:T(8,128)}, f32[256,64]{1,0:T(8,128)}), (f32[128,1600]{1,0:T(8,128)}, f32[256,64]{1,0:T(8,128)})) %all-reduce.4.cloned.1.call-update) | async-done | bytes 884752 | tf_op jit(solution)/shard_map/psum | solution.py:155
  372.2 1.4 constant_dynamic-slice_fusion
  373.6 1.2 constant_dynamic-slice_fusion.3
  (91 shorter events, 7.2 us)
Async XLA Ops:
  7.2 4.7 %copy-start = (bf16[2,64,1024]{2,1,0:T(8,128)(2,1)S(1)}, bf16[2,64,1024]{2,1,0:T(8,128)(2,1)}, u32[]{:S(2)}) copy-start(bf16[2,64,1024]{2,1,0:T(8,128)(2,1)} %param.11) | copy-start | bytes 786436
  7.2 5.9 %copy-start.10 = (bf16[1,2,64,4096]{3,2,1,0:T(8,128)(2,1)S(1)}, bf16[1,2,64,4096]{3,2,1,0:T(8,128)(2,1)}, u32[]{:S(2)}) copy-start(bf16[1,2,64,4096]{3,2,1,0:T(8,128)(2,1)} %param.10) | copy-start | bytes 3145732
  7.2 75.5 %collective-permute-start = (bf16[2,1024]{1,0:T(2,128)(2,1)}, bf16[2,1024]{1,0:T(2,128)(2,1)S(1)}, u32[]{:S(2)}, u32[]{:S(2)}) collective-permute-start(bf16[2,1024]{1,0:T(2,128)(2,1)} %bitcast.89), channel_id=1, source_target_pairs={{0,2},{2,0},{4,6},{6,4},{8,10},{10,8},{12,14},{14,12},{16,18},{18,... | collective-permute-start | bytes 12296 | tf_op jit(solution)/shard_map/ppermute | solution.py:9
  24.4 6.9 %copy-start.15 = (f32[256,64]{0,1:T(8,128)S(1)}, f32[256,64]{0,1:T(8,128)}, u32[]{:S(2)}) copy-start(f32[256,64]{0,1:T(8,128)} %param.13) | copy-start | bytes 196612
  24.4 7.1 %copy-start.11 = (bf16[64,64,4,4]{1,0,3,2:T(8,128)(2,1)S(1)}, bf16[64,64,4,4]{1,0,3,2:T(8,128)(2,1)}, u32[]{:S(2)}) copy-start(bf16[64,64,4,4]{1,0,3,2:T(8,128)(2,1)} %copy.169) | copy-start | bytes 393220
  24.4 7.1 %copy-start.17 = (pred[16,5]{0,1:T(8,128)(4,1)S(1)}, pred[16,5]{0,1:T(8,128)(4,1)}, u32[]{:S(2)}) copy-start(pred[16,5]{0,1:T(8,128)(4,1)} %constant.131) | copy-start | bytes 244
  36.3 2.8 copy-start.8
  36.3 1.1 copy-start.13
  40.3 16.9 %collective-permute-start.1 = (bf16[2,64,1024]{1,2,0:T(8,128)(2,1)}, bf16[2,64,1024]{1,2,0:T(8,128)(2,1)}, u32[]{:S(2)}, u32[]{:S(2)}) collective-permute-start(bf16[2,64,1024]{1,2,0:T(8,128)(2,1)} %bitcast.12), channel_id=1, source_target_pairs={{0,2},{2,0},{4,6},{6,4},{8,10},{10,8},{12,14},{14,12},{16,18},{18,... | collective-permute-start | bytes 786440 | tf_op jit(solution)/shard_map/ppermute | solution.py:9
  41.6 3.6 copy-start.21
  41.6 4.9 %copy-start.18 = (s32[64,4]{0,1:T(4,128)S(1)}, s32[64,4]{0,1:T(4,128)}, u32[]{:S(2)}) copy-start(s32[64,4]{0,1:T(4,128)} %param.15) | copy-start | bytes 3076
  52.3 1.6 copy-start.2
  57.3 9.1 %copy-start.16 = (bf16[1,2,1024]{2,1,0:T(2,128)(2,1)S(1)}, bf16[1,2,1024]{2,1,0:T(2,128)(2,1)}, u32[]{:S(2)}) copy-start(bf16[1,2,1024]{2,1,0:T(2,128)(2,1)} %param.14) | copy-start | bytes 12292
  62.0 27.2 %all-to-all-start = ((bf16[2,2,64,1024]{3,2,1,0:T(8,128)(2,1)}), bf16[2,2,64,1024]{3,2,1,0:T(8,128)(2,1)}, u32[]{:S(2)}, u32[]{:S(2)}) async-start(bf16[2,2,64,1024]{3,2,1,0:T(8,128)(2,1)} %copy.174), calls=%async_computation | async-start | bytes 1048576 | tf_op jit(solution)/shard_map/all_to_all | solution.py:96
  66.2 305.9 %all-reduce.4.cloned.1.call-start = ((), (), s32[]{:S(2)}) async-start(), calls=%async_computation.1 | async-start | bytes 1966080 | tf_op jit(solution)/shard_map/psum | solution.py:155
  74.9 4.8 %copy-start.3 = (bf16[64,64,2,8,10]{1,0,4,3,2:T(8,128)(2,1)S(1)}, bf16[64,64,2,8,10]{1,0,4,3,2:T(8,128)(2,1)}, u32[]{:S(2)}) copy-start(bf16[64,64,2,8,10]{1,0,4,3,2:T(8,128)(2,1)} %fusion.17) | copy-start | bytes 3932164
  95.5 1.3 copy-start.9
  95.5 1.3 copy-start.14
  96.8 2.2 copy-start.5
  96.8 2.5 copy-start.6
  96.8 3.3 copy-start.7
  98.3 2.8 copy-start.4
  101.1 5.5 %copy-start.19 = (pred[256]{0:T(512)(128)(4,1)S(1)}, pred[256]{0:T(512)(128)(4,1)}, u32[]{:S(2)}) copy-start(pred[256]{0:T(512)(128)(4,1)} %iota_compare_fusion.9) | copy-start | bytes 772
  106.1 1.6 copy-start.20
  107.4 1.3 copy-start.12
  112.4 262.4 %copy-start.1 = (bf16[2,64,1024]{2,1,0:T(8,128)(2,1)S(1)}, bf16[2,64,1024]{2,1,0:T(8,128)(2,1)}, u32[]{:S(2)}) copy-start(bf16[2,64,1024]{2,1,0:T(8,128)(2,1)} %param.11) | copy-start | bytes 786436
Sparse Core Ops, SparseCore 0:
  108.9 263.2 all-reduce.3
